TPU v7x, 128 devices: a whole 4x4x4 slice. The times are simulated.
128 devices in a mesh: fx: 8 (over y_hi, z), fy: 16 (over x, y_lo, core).
Axes of the slice: x: 4, y: 4 (y_hi: 2, y_lo: 2; y = y_hi * 2 + y_lo), z: 4, core: 2. Of those that a mesh axis runs over, the one named last changes fastest.
Arguments:
- facets: float32 [8192, 4096], P('fx', 'fy'), may hold values from -6 to 6
- counts: int32 [8, 16], P('fx', 'fy'), may hold values from 1 to 16, as said below
- cells: int32 [2, 8, 16, 2048], P(None, 'fx', 'fy'), may hold values from 0 to 248
- fracs: float32 [2, 8, 16, 2048], P(None, 'fx', 'fy'), may hold values from 0 to 1
Outputs:
- predictions: float32 [2, 8, 16, 2048], P(None, 'fx', 'fy')
Inputs may be any that keep to these rules, and one draw needn't show every extreme that they name: Blocks 0 to counts - 1 of a subgrid's 128-visibility blocks are live, the others are padding; some subgrid has 16 live blocks.
All inputs are finite; a program needn't handle non-finite values.
Results may differ from a plain program's by a relative error of at most 0.0003.
Values sent between devices are 32-bit elements; how exact they have to be, the bound alone decides.
A program may use at most 128 MiB of HBM per device.

v0:
```python
import math
import jax
import jax.numpy as jnp
from jax import lax
from jax.sharding import Mesh
from jax.sharding import PartitionSpec as P

NIMG = 65536
FP = 4096
SUBGRID = 256
SUPPORT = 8
VBLOCK = 128
FX = ("fx_0", "fx_1")


def sum_in_order(blocks, axes, turns):
    dims = [lax.axis_size(a) for a in axes]
    blocks = blocks.reshape(*dims, *blocks.shape[1:])
    blocks = blocks.transpose(*turns, *range(len(axes), blocks.ndim))
    blocks = blocks.reshape(-1, *blocks.shape[len(axes) :])
    for k in turns:
        blocks = lax.psum_scatter(blocks, axes[k], scatter_dimension=0, tiled=True)
    return blocks[0]


def split_up(array, dim, length):
    before, after = (array.shape[:dim], array.shape[dim + 1 :])
    return jnp.moveaxis(array.reshape(*before, length, -1, *after), dim, 0)


def summed_rows(array, axes, turns, dim):
    length = lax.axis_size(axes)
    return sum_in_order(split_up(array, dim, length), axes, turns)


def mulmod(upper, lower):
    low = upper % 256
    high = upper // 256
    return (low * lower + 256 * (high * lower % (NIMG // 256))) % NIMG


def factor(freqs, pixels, scale):
    inner = pixels % FP
    turns = mulmod(freqs[:, None], pixels[None, :])
    angle = turns.astype(jnp.float32) * (2.0 * math.pi / NIMG)
    window = jnp.sin(math.pi * (inner.astype(jnp.float32) + 0.5) / FP) * scale
    return (jnp.cos(angle) * window[None, :], -jnp.sin(angle) * window[None, :])


def kernel(offset, frac):
    positions = jnp.arange(SUBGRID, dtype=jnp.int32)
    dist = positions[None, :] - offset[:, None]
    inside = (dist >= 0) & (dist < SUPPORT)
    shift = dist.astype(jnp.float32) - (SUPPORT // 2 - 1) - frac[:, None]
    value = 0.6 * jnp.exp(-shift * shift / 4.5)
    return jnp.where(inside, value, jnp.zeros_like(value))


def column_term(v_start, v_count, p_real, p_imag, columns, scale):
    freqs = v_start * SUBGRID + jnp.arange(v_count * SUBGRID, dtype=jnp.int32)
    b_real, b_imag = factor(freqs, columns, scale)
    left = jnp.concatenate([b_real, b_imag], axis=0)
    right = jnp.concatenate([p_real, p_imag], axis=0)
    product = lax.dot_general(
        left,
        right,
        (((1,), (1,)), ((), ())),
        precision=lax.Precision.HIGHEST,
        preferred_element_type=jnp.float32,
    )
    height = v_count * SUBGRID
    width = p_real.shape[0]
    t_real = product[:height, :width] - product[height:, width:]
    t_imag = product[height:, :width] + product[:height, width:]
    return jnp.stack(
        [t_real.reshape(v_count, SUBGRID, width), t_imag.reshape(v_count, SUBGRID, width)], axis=1
    )


def degrid(values, grid, cell_rows, frac_rows, row, col, stride, turns):
    highest = lax.Precision.HIGHEST

    def step(turn, values):
        offset = stride * turn * VBLOCK
        cells_u = lax.dynamic_slice_in_dim(cell_rows[0], offset, VBLOCK)
        cells_v = lax.dynamic_slice_in_dim(cell_rows[1], offset, VBLOCK)
        fracs_u = lax.dynamic_slice_in_dim(frac_rows[0], offset, VBLOCK)
        fracs_v = lax.dynamic_slice_in_dim(frac_rows[1], offset, VBLOCK)
        weight_u = kernel(cells_u, fracs_u)
        weight_v = kernel(cells_v, fracs_v)
        g_real = jnp.dot(weight_v, grid[0], precision=highest, preferred_element_type=jnp.float32)
        g_imag = jnp.dot(weight_v, grid[1], precision=highest, preferred_element_type=jnp.float32)
        block = jnp.stack([jnp.sum(g_real * weight_u, axis=1), jnp.sum(g_imag * weight_u, axis=1)])
        zero = jnp.zeros((), jnp.int32)
        return lax.dynamic_update_slice(
            values, block[:, None, None, :], (zero, jnp.int32(row), jnp.int32(col), offset)
        )

    return lax.fori_loop(jnp.int32(0), turns, step, values)


def per_device(facets, counts, cells, fracs):
    highest = lax.Precision.HIGHEST
    su_dev = counts.shape[0]
    sv_dev = counts.shape[1]
    local_rows = facets.shape[0]
    local_cols = facets.shape[1]
    row_scale = math.sqrt(2.0 / (local_rows * lax.axis_size(FX)))
    col_scale = math.sqrt(2.0 / (local_cols * lax.axis_size("fy")))
    row_index = lax.axis_index(FX)
    col_index = lax.axis_index("fy")
    my_rows = row_index * local_rows + jnp.arange(local_rows, dtype=jnp.int32)
    count = su_dev * lax.axis_size(FX)
    freqs = jnp.arange(count * SUBGRID, dtype=jnp.int32)
    real_part, imag_part = factor(freqs, my_rows, row_scale)
    table = jnp.stack(
        [
            real_part.reshape(count, SUBGRID, local_rows),
            imag_part.reshape(count, SUBGRID, local_rows),
        ],
        axis=1,
    )
    product = jnp.dot(
        table.reshape(count * 2 * SUBGRID, local_rows),
        facets,
        precision=highest,
        preferred_element_type=jnp.float32,
    )
    partial_sums = summed_rows(product.reshape(count, 2, SUBGRID, local_cols), FX, (1, 0), 0)
    piece = lax.all_gather(partial_sums, "fy", axis=3, tiled=True)
    width = piece.shape[3]
    columns = jnp.arange(width, dtype=jnp.int32)
    term = column_term(
        col_index * sv_dev,
        sv_dev,
        piece[:, 0].reshape(su_dev * SUBGRID, width),
        piece[:, 1].reshape(su_dev * SUBGRID, width),
        columns,
        col_scale,
    )
    blank = jnp.zeros((2, su_dev, sv_dev, cells.shape[3]), jnp.float32)
    values = blank
    grid = term[0, :, :, 0:SUBGRID]
    values = degrid(values, grid, cells[:, 0, 0], fracs[:, 0, 0], 0, 0, 1, counts[0, 0])
    return values


def solution(mesh):
    torus = Mesh(mesh.devices.reshape(2, 4, mesh.shape["fy"]), ("fx_0", "fx_1", "fy"))
    in_specs = (P(FX, "fy"), P(FX, "fy"), P(None, FX, "fy", None), P(None, FX, "fy", None))
    out_specs = P(None, FX, "fy", None)
    return jax.shard_map(
        per_device, mesh=torus, in_specs=in_specs, out_specs=out_specs, check_vma=False
    )
```

profile of v0, /device:TPU:43, one launch (start us, length us, event | category | flops | bytes accessed | tf_op | source)
XLA Modules:
  0.0 245.5 jit_solution(14438846253240212937)
XLA Ops:
  6.6 0.1 add_select_fusion.6
  6.7 37.7 %cosine_multiply_fusion = (f32[2,4,1,256,1024]{4,3,2,1,0:T(8,128)S(1)}, f32[2,4,1,256,1024]{4,3,2,1,0:T(8,128)S(1)}) fusion(f32[1024]{0:T(1024)S(1)} %fusion.104, s32[2,4,256]{2,1,0:T(4,128)S(1)} %get-tuple-element.134, s32[1024]{0:T(1024)S(1)} %iota_add_fusion.1, s32[2,4,256]{2,1,0:T(4,128)S(1)} %get-tuple-element.133), kind=kLoop, calls=%fused_computation.90 | loop fusion | flops 65011712 | bytes 16801792 | tf_op jit(solution)/shard_map/mul | solution.py:47
  44.4 14.9 %fusion.80 = f32[4,2,1,2,256,256]{5,4,3,0,1,2:T(8,128)S(1)} fusion(f32[2,4,1,256,1024]{4,3,2,1,0:T(8,128)S(1)} %get-tuple-element.130, f32[2,4,1,256,1024]{4,3,2,1,0:T(8,128)S(1)} %get-tuple-element.129, f32[1024,256]{1,0:T(8,128)S(1)} %copy-done), kind=kOutput, calls=%fused_computation.110 | convolution fusion | flops 12889096192 | bytes 22020096 | tf_op jit(solution)/shard_map/dot_general | solution.py:123
  59.4 2.4 copy.6
  61.8 47.6 %reduce-scatter.3.cloned.1.call-done = f32[2,1,2,256,256]{4,3,2,0,1:T(8,128)} async-done(((f32[8,1,2,256,256]{4,3,2,0,1:T(8,128)}), f32[2,1,2,256,256]{4,3,2,0,1:T(8,128)}) %reduce-scatter.3.cloned.1.call-update) | async-done | bytes 1048592 | tf_op jit(solution)/shard_map/reduce_scatter | solution.py:22
  109.5 26.7 %reduce-scatter.5.cloned.1.call-done = f32[1,1,2,256,256]{4,3,2,0,1:T(8,128)} async-done(((f32[2,1,2,256,256]{4,3,2,0,1:T(8,128)}), f32[1,1,2,256,256]{4,3,2,0,1:T(8,128)}) %reduce-scatter.5.cloned.1.call-update) | async-done | bytes 524304 | tf_op jit(solution)/shard_map/reduce_scatter | solution.py:22
  136.3 0.1 fusion.90
  136.4 20.3 %cosine_multiply_fusion.1 = (f32[256,4096]{1,0:T(8,128)}, f32[256,4096]{1,0:T(8,128)}) fusion(f32[4096]{0:T(1024)S(1)} %fusion.90, s32[256]{0:T(256)S(1)} %get-tuple-element.135, s32[256]{0:T(256)S(1)} %get-tuple-element.136), kind=kLoop, calls=%fused_computation.106 | loop fusion | flops 32505856 | bytes 8407040 | tf_op jit(solution)/shard_map/mul | solution.py:47
  156.7 34.1 %all-gather.3.cloned.1.call-done = f32[1,1,2,256,4096]{4,3,2,0,1:T(8,128)} async-done(((f32[1,1,2,256,256]{4,3,2,0,1:T(8,128)}), f32[1,1,2,256,4096]{4,3,2,0,1:T(8,128)}) %all-gather.3.cloned.1.call-update) | async-done | bytes 8388624 | tf_op jit(solution)/shard_map/all_gather | solution.py:130
  190.8 4.1 %slice_bitcast_fusion.1 = (f32[256,4096]{1,0:T(8,128)S(1)}, f32[256,4096]{1,0:T(8,128)S(1)}) fusion(f32[1,2,256,4096]{3,2,1,0:T(8,128)} %bitcast.62), kind=kLoop, calls=%fused_computation.104 | loop fusion | bytes 16777216 | tf_op jit(solution)/shard_map/reshape;squeeze | solution.py:136
  195.0 0.5 copy-done.1
  195.5 1.3 copy-done.2
  196.7 14.3 %fusion.64 = f32[512,512]{1,0:T(8,128)S(1)} fusion(f32[256,4096]{1,0:T(8,128)S(1)} %copy-done.2, f32[256,4096]{1,0:T(8,128)S(1)} %copy-done.1, f32[256,4096]{1,0:T(8,128)S(1)} %get-tuple-element.126, f32[256,4096]{1,0:T(8,128)S(1)} %get-tuple-element.125), kind=kOutput, calls=%fused_computation.82 | convolution fusion | flops 12889096192 | bytes 17825792 | tf_op jit(solution)/shard_map/dot_general | solution.py:64
  211.1 0.1 fusion.85
  211.2 27.2 %while.13 = (s32[]{:T(128)}, f32[2,1,1,2048]{3,2,1,0:T(1,128)S(1)}, s32[]{:T(128)}, s32[2,2048]{1,0:T(2,128)S(1)}, f32[2,2048]{1,0:T(2,128)S(1)}, /*index=5*/f32...) while((s32[]{:T(128)}, f32[2,1,1,2048]{3,2,1,0:T(1,128)S(1)}, s32[]{:T(128)}, ...), condition=%wide.region_5.6_spmd, body=%wide.region_2.5_spmd.sunk | while | flops 203030528 | bytes 603295 | solution.py:99
  211.9 0.4 fusion.129
  212.4 0.4 fusion.128
  213.6 0.4 fusion.129
  214.0 0.4 fusion.128
  215.3 0.4 fusion.129
  215.7 0.4 fusion.128
  216.9 0.4 fusion.129
  217.4 0.4 fusion.128
  218.6 0.4 fusion.129
  219.0 0.4 fusion.128
  220.2 0.4 fusion.129
  220.7 0.4 fusion.128
  221.9 0.4 fusion.129
  222.3 0.4 fusion.128
  223.6 0.4 fusion.129
  224.0 0.4 fusion.128
  225.2 0.4 fusion.129
  225.7 0.4 fusion.128
  226.9 0.4 fusion.129
  227.3 0.4 fusion.128
  228.5 0.4 fusion.129
  229.0 0.4 fusion.128
  230.2 0.4 fusion.129
  230.6 0.4 fusion.128
  231.8 0.4 fusion.129
  232.3 0.4 fusion.128
  233.5 0.4 fusion.129
  233.9 0.4 fusion.128
  235.2 0.4 fusion.129
  235.6 0.4 fusion.128
  236.8 0.4 fusion.129
  237.3 0.4 fusion.128
  238.4 0.6 copy-done.5
  (119 shorter events, 1.5 us)
Async XLA Ops:
  6.5 37.9 %copy-start = (f32[1024,256]{1,0:T(8,128)S(1)}, f32[1024,256]{1,0:T(8,128)}, u32[]{:S(2)}) copy-start(f32[1024,256]{1,0:T(8,128)} %param.6) | copy-start | bytes 3145732
  6.5 102.9 %reduce-scatter.3.cloned.1.call-start = ((), (), s32[]{:S(2)}) async-start(), calls=%async_computation.2 | async-start | bytes 5242880 | tf_op jit(solution)/shard_map/reduce_scatter | solution.py:22
  61.7 74.5 %copy-start.3 = (f32[2,1,1,2048]{3,2,1,0:T(1,128)S(1)}, f32[2,1,1,2048]{3,2,1,0:T(1,128)}, u32[]{:S(2)}) copy-start(f32[2,1,1,2048]{3,2,1,0:T(1,128)} %param.9) | copy-start | bytes 49156
  61.7 74.5 %copy-start.4 = (s32[2,1,1,2048]{3,2,1,0:T(1,128)S(1)}, s32[2,1,1,2048]{3,2,1,0:T(1,128)}, u32[]{:S(2)}) copy-start(s32[2,1,1,2048]{3,2,1,0:T(1,128)} %param.8) | copy-start | bytes 49156
  61.8 74.5 %reduce-scatter.5.cloned.1.call-start = ((), (), s32[]{:S(2)}) async-start(), calls=%async_computation.3 | async-start | bytes 1572864 | tf_op jit(solution)/shard_map/reduce_scatter | solution.py:22
  109.5 81.4 %all-gather.3.cloned.1.call-start = ((), (), s32[]{:S(2)}) async-start(), calls=%async_computation.4 | async-start | bytes 8912896 | tf_op jit(solution)/shard_map/all_gather | solution.py:130
  190.8 4.6 %copy-start.1 = (f32[256,4096]{1,0:T(8,128)S(1)}, f32[256,4096]{1,0:T(8,128)}, u32[]{:S(2)}) copy-start(f32[256,4096]{1,0:T(8,128)} %get-tuple-element.131) | copy-start | bytes 12582916
  190.8 5.9 %copy-start.2 = (f32[256,4096]{1,0:T(8,128)S(1)}, f32[256,4096]{1,0:T(8,128)}, u32[]{:S(2)}) copy-start(f32[256,4096]{1,0:T(8,128)} %get-tuple-element.132) | copy-start | bytes 12582916
  238.4 0.6 copy-start.5
Sparse Core Ops, SparseCore 0:
  61.9 47.4 reduce-scatter.2
  111.8 24.3 reduce-scatter.4
  137.9 52.8 all-gather.2
where the time goes:
time: 246 us
  waiting for transfers between devices  108 us (44%)
  other arithmetic  58.5 us (24%)
  matrix products  43.3 us (18%)
  between operations  13.2 us (5%)
  loops' own time  11.9 us (5%)
  local copies, waits for them, and re-layouts  9.97 us (4%)
    reduce_scatter x2, waiting for transfers between devices, sum_in_order(): blocks = lax.psum_scatter(blocks, axes[k], scatter_dimension=0, tiled=True)  74.3 us
    mul x2, other arithmetic, factor(): return (jnp.cos(angle) * window[None, :], -jnp.sin(angle) * window[None, :])  58 us
    all_gather x1, waiting for transfers between devices, per_device(): piece = lax.all_gather(partial_sums, 'fy', axis=3, tiled=True)  34.1 us
    dot_general x1, matrix products, per_device(): jnp.dot(table.reshape(count * 2 * SUBGRID, local_rows), facets, precision...  14.9 us
    dot_general x1, matrix products, column_term(): lax.dot_general(left, right, (((1,), (1,)), ((), ())), precision=lax.Prec...  14.3 us
    another operation x1, loops' own time, degrid(): return lax.fori_loop(jnp.int32(0), turns, step, values)  11.9 us
    dot_general x16, matrix products, step(): jnp.dot(weight_v, grid[1], precision=highest, preferred_element_type=jnp....  7.06 us
    dot_general x16, matrix products, step(): jnp.dot(weight_v, grid[0], precision=highest, preferred_element_type=jnp....  6.98 us
  transfers between devices with their start and end apart: 3, of which 3 were waited for; matrix products, arithmetic and copies ran while one was open for 8% of the time, Pallas kernels for 0%

commit v1 on v0

--- a/solution.py
+++ b/solution.py
@@ -11,6 +11,12 @@
 SUPPORT = 8
 VBLOCK = 128
 FX = ("fx_0", "fx_1")
+
+
+def gather_blocks(x, axis, dim):
+    blocks = lax.all_gather(x, axis, axis=0, tiled=False)
+    whole = jnp.concatenate(blocks, axis=dim)
+    return whole
 
 
 def sum_in_order(blocks, axes, turns):
@@ -127,7 +133,7 @@
         preferred_element_type=jnp.float32,
     )
     partial_sums = summed_rows(product.reshape(count, 2, SUBGRID, local_cols), FX, (1, 0), 0)
-    piece = lax.all_gather(partial_sums, "fy", axis=3, tiled=True)
+    piece = gather_blocks(partial_sums, "fy", 3)
     width = piece.shape[3]
     columns = jnp.arange(width, dtype=jnp.int32)
     term = column_term(

time: 246 us -> 254 us (1.033)
  local copies, waits for them, and re-layouts: 9.97 us -> 18.6 us
    all_gather x0 -> x1, local copies, waits for them, and re-layouts: none -> 8.67 us  [gather_blocks(): blocks = lax.all_gather(x, axis, axis=0, tiled=False)]
where the time goes in v1:
time: 254 us
  waiting for transfers between devices  109 us (43%)
  other arithmetic  58.5 us (23%)
  matrix products  43.1 us (17%)
  local copies, waits for them, and re-layouts  18.6 us (7%)
  between operations  13.3 us (5%)
  loops' own time  11.9 us (5%)
    reduce_scatter x2, waiting for transfers between devices, sum_in_order(): blocks = lax.psum_scatter(blocks, axes[k], scatter_dimension=0, tiled=True)  74.3 us
    mul x2, other arithmetic, factor(): return (jnp.cos(angle) * window[None, :], -jnp.sin(angle) * window[None, :])  58 us
    all_gather x1, waiting for transfers between devices, gather_blocks(): blocks = lax.all_gather(x, axis, axis=0, tiled=False)  34.1 us
    dot_general x1, matrix products, per_device(): jnp.dot(table.reshape(count * 2 * SUBGRID, local_rows), facets, precision...  14.9 us
    dot_general x1, matrix products, column_term(): lax.dot_general(left, right, (((1,), (1,)), ((), ())), precision=lax.Prec...  14.1 us
    another operation x1, loops' own time, degrid(): return lax.fori_loop(jnp.int32(0), turns, step, values)  11.9 us
    all_gather x1, local copies, waits for them, and re-layouts, gather_blocks(): blocks = lax.all_gather(x, axis, axis=0, tiled=False)  8.67 us
    dot_general x16, matrix products, step(): jnp.dot(weight_v, grid[1], precision=highest, preferred_element_type=jnp....  7.06 us
  transfers between devices with their start and end apart: 3, of which 3 were waited for; matrix products, arithmetic and copies ran while one was open for 8% of the time, Pallas kernels for 0%

profile of v1, /device:TPU:43, one launch (start us, length us, event | category | flops | bytes accessed | tf_op | source)
XLA Modules:
  0.0 254.1 jit_solution(16233136711125162758)
XLA Ops:
  6.6 0.1 add_select_fusion.6
  6.7 37.7 %cosine_multiply_fusion = (f32[2,4,1,256,1024]{4,3,2,1,0:T(8,128)S(1)}, f32[2,4,1,256,1024]{4,3,2,1,0:T(8,128)S(1)}) fusion(f32[1024]{0:T(1024)S(1)} %fusion.104, s32[2,4,256]{2,1,0:T(4,128)S(1)} %get-tuple-element.134, s32[1024]{0:T(1024)S(1)} %iota_add_fusion.1, s32[2,4,256]{2,1,0:T(4,128)S(1)} %get-tuple-element.133), kind=kLoop, calls=%fused_computation.90 | loop fusion | flops 65011712 | bytes 16801792 | tf_op jit(solution)/shard_map/mul | solution.py:53
  44.4 14.9 %fusion.80 = f32[4,2,1,2,256,256]{5,4,3,0,1,2:T(8,128)S(1)} fusion(f32[2,4,1,256,1024]{4,3,2,1,0:T(8,128)S(1)} %get-tuple-element.130, f32[2,4,1,256,1024]{4,3,2,1,0:T(8,128)S(1)} %get-tuple-element.129, f32[1024,256]{1,0:T(8,128)S(1)} %copy-done), kind=kOutput, calls=%fused_computation.110 | convolution fusion | flops 12889096192 | bytes 22020096 | tf_op jit(solution)/shard_map/dot_general | solution.py:129
  59.4 2.4 copy.9
  61.8 47.6 %reduce-scatter.3.cloned.1.call-done = f32[2,1,2,256,256]{4,3,2,0,1:T(8,128)} async-done(((f32[8,1,2,256,256]{4,3,2,0,1:T(8,128)}), f32[2,1,2,256,256]{4,3,2,0,1:T(8,128)}) %reduce-scatter.3.cloned.1.call-update) | async-done | bytes 1048592 | tf_op jit(solution)/shard_map/reduce_scatter | solution.py:28
  109.5 26.7 %reduce-scatter.5.cloned.1.call-done = f32[1,1,2,256,256]{4,3,2,0,1:T(8,128)} async-done(((f32[2,1,2,256,256]{4,3,2,0,1:T(8,128)}), f32[1,1,2,256,256]{4,3,2,0,1:T(8,128)}) %reduce-scatter.5.cloned.1.call-update) | async-done | bytes 524304 | tf_op jit(solution)/shard_map/reduce_scatter | solution.py:28
  136.3 0.1 fusion.90
  136.4 20.3 %cosine_multiply_fusion.1 = (f32[256,4096]{1,0:T(8,128)}, f32[256,4096]{1,0:T(8,128)}) fusion(f32[4096]{0:T(1024)S(1)} %fusion.90, s32[256]{0:T(256)S(1)} %get-tuple-element.135, s32[256]{0:T(256)S(1)} %get-tuple-element.136), kind=kLoop, calls=%fused_computation.106 | loop fusion | flops 32505856 | bytes 8407040 | tf_op jit(solution)/shard_map/mul | solution.py:53
  156.7 34.1 %all-gather.2.cloned.1.call-done = f32[16,1,2,256,256]{4,3,2,1,0:T(8,128)} async-done(((f32[1,1,2,256,256]{4,3,2,1,0:T(8,128)}), f32[16,1,2,256,256]{4,3,2,1,0:T(8,128)}) %all-gather.2.cloned.1.call-update) | async-done | bytes 8388624 | tf_op jit(solution)/shard_map/all_gather | solution.py:17
  190.9 8.7 %copy.11 = f32[16,1,2,256,256]{3,4,0,2,1:T(8,128)} copy(f32[16,1,2,256,256]{4,3,2,1,0:T(8,128)} %all-gather.2.cloned.1.call-done) | data formatting | bytes 16777216 | tf_op jit(solution)/shard_map/all_gather | solution.py:17
  199.5 4.2 %slice_bitcast_fusion.1 = (f32[256,4096]{0,1:T(8,128)S(1)}, f32[256,4096]{0,1:T(8,128)S(1)}) fusion(f32[1,2,256,4096]{2,3,1,0:T(8,128)} %bitcast.64), kind=kLoop, calls=%fused_computation.104 | loop fusion | bytes 16777216 | tf_op jit(solution)/shard_map/reshape;squeeze | solution.py:142
  203.7 0.5 copy-done.1
  204.2 1.3 copy-done.2
  205.4 14.1 %fusion.64 = f32[512,512]{1,0:T(8,128)S(1)} fusion(f32[256,4096]{1,0:T(8,128)S(1)} %copy-done.2, f32[256,4096]{1,0:T(8,128)S(1)} %copy-done.1, f32[256,4096]{0,1:T(8,128)S(1)} %get-tuple-element.126, f32[256,4096]{0,1:T(8,128)S(1)} %get-tuple-element.125), kind=kOutput, calls=%fused_computation.82 | convolution fusion | flops 12889096192 | bytes 17825792 | tf_op jit(solution)/shard_map/dot_general | solution.py:70
  219.7 27.2 %while.13 = (s32[]{:T(128)}, f32[2,1,1,2048]{3,2,1,0:T(1,128)S(1)}, s32[]{:T(128)}, s32[2,2048]{1,0:T(2,128)S(1)}, f32[2,2048]{1,0:T(2,128)S(1)}, /*index=5*/f32...) while((s32[]{:T(128)}, f32[2,1,1,2048]{3,2,1,0:T(1,128)S(1)}, s32[]{:T(128)}, ...), condition=%wide.region_5.6_spmd, body=%wide.region_2.5_spmd.sunk | while | flops 203030528 | bytes 603295 | solution.py:105
  220.5 0.4 fusion.129
  220.9 0.4 fusion.128
  222.1 0.4 fusion.129
  222.6 0.4 fusion.128
  223.8 0.4 fusion.129
  224.2 0.4 fusion.128
  225.4 0.4 fusion.129
  225.9 0.4 fusion.128
  227.1 0.4 fusion.129
  227.5 0.4 fusion.128
  228.8 0.4 fusion.129
  229.2 0.4 fusion.128
  230.4 0.4 fusion.129
  230.9 0.4 fusion.128
  232.1 0.4 fusion.129
  232.5 0.4 fusion.128
  233.7 0.4 fusion.129
  234.2 0.4 fusion.128
  235.4 0.4 fusion.129
  235.8 0.4 fusion.128
  237.1 0.4 fusion.129
  237.5 0.4 fusion.128
  238.7 0.4 fusion.129
  239.2 0.4 fusion.128
  240.4 0.4 fusion.129
  240.8 0.4 fusion.128
  242.0 0.4 fusion.129
  242.5 0.4 fusion.128
  243.7 0.4 fusion.129
  244.1 0.4 fusion.128
  245.4 0.4 fusion.129
  245.8 0.4 fusion.128
  246.9 0.6 copy-done.5
  (120 shorter events, 1.6 us)
Async XLA Ops:
  6.5 37.9 %copy-start = (f32[1024,256]{1,0:T(8,128)S(1)}, f32[1024,256]{1,0:T(8,128)}, u32[]{:S(2)}) copy-start(f32[1024,256]{1,0:T(8,128)} %param.6) | copy-start | bytes 3145732
  6.5 102.9 %reduce-scatter.3.cloned.1.call-start = ((), (), s32[]{:S(2)}) async-start(), calls=%async_computation.2 | async-start | bytes 5242880 | tf_op jit(solution)/shard_map/reduce_scatter | solution.py:28
  61.7 74.5 %copy-start.3 = (f32[2,1,1,2048]{3,2,1,0:T(1,128)S(1)}, f32[2,1,1,2048]{3,2,1,0:T(1,128)}, u32[]{:S(2)}) copy-start(f32[2,1,1,2048]{3,2,1,0:T(1,128)} %param.9) | copy-start | bytes 49156
  61.7 74.5 %copy-start.4 = (s32[2,1,1,2048]{3,2,1,0:T(1,128)S(1)}, s32[2,1,1,2048]{3,2,1,0:T(1,128)}, u32[]{:S(2)}) copy-start(s32[2,1,1,2048]{3,2,1,0:T(1,128)} %param.8) | copy-start | bytes 49156
  61.8 74.5 %reduce-scatter.5.cloned.1.call-start = ((), (), s32[]{:S(2)}) async-start(), calls=%async_computation.3 | async-start | bytes 1572864 | tf_op jit(solution)/shard_map/reduce_scatter | solution.py:28
  109.5 81.4 %all-gather.2.cloned.1.call-start = ((), (), s32[]{:S(2)}) async-start(), calls=%async_computation.4 | async-start | bytes 8912896 | tf_op jit(solution)/shard_map/all_gather | solution.py:17
  199.5 4.6 %copy-start.1 = (f32[256,4096]{1,0:T(8,128)S(1)}, f32[256,4096]{1,0:T(8,128)}, u32[]{:S(2)}) copy-start(f32[256,4096]{1,0:T(8,128)} %get-tuple-element.131) | copy-start | bytes 12582916
  199.5 5.9 %copy-start.2 = (f32[256,4096]{1,0:T(8,128)S(1)}, f32[256,4096]{1,0:T(8,128)}, u32[]{:S(2)}) copy-start(f32[256,4096]{1,0:T(8,128)} %get-tuple-element.132) | copy-start | bytes 12582916
  246.9 0.6 copy-start.5
Sparse Core Ops, SparseCore 0:
  61.9 47.4 reduce-scatter.2
  111.8 24.3 reduce-scatter.4
  137.9 52.8 all-gather.1
